TPU v7x, 32 devices: a whole 2x2x4 slice. The times are simulated.
32 devices in a mesh: shape: 8 (over z, x), cls: 4 (over y, core).
Axes of the slice: x: 2, y: 2, z: 4, core: 2. Of those that a mesh axis runs over, the one named last changes fastest.
Arguments:
- shapes: bfloat16 [4096, 1280], P('shape', 'cls'), may hold values from -600 to 600
- classes: bfloat16 [20480, 1280], P('cls'), may hold values from -400 to 400
- counts: int32 [20480], P('cls'), may hold values from 0 to 2, as said below
Outputs:
- assignment: bfloat16 [4096, 20480], P('shape', 'cls')
Inputs may be any that keep to these rules, and one draw needn't show every extreme that they name: The counts sum to 4096; exactly 1024 classes have count 2.
All inputs are finite; a program needn't handle non-finite values.
Results may differ from a plain program's by a relative error of at most 0.001.
Values may be sent and summed in bfloat16 or wider, within the bound.
No kernel may reach another device: no remote copies, remote signals or barrier semaphores. Data moves between devices by JAX's collectives and lax.ppermute only.
A program may use at most 128 MiB of HBM per device.

v0:
```python
import jax
import jax.numpy as jnp
from jax import lax
from jax.sharding import PartitionSpec as P

ITERS = 3
logit_scale = 40.0
epsilon = 1e-06


def row_totals(partial_value):
    return lax.psum(partial_value, "cls")


def shards(shapes, classes, counts):
    class_f = classes.astype(jnp.float32)
    class_scale = lax.rsqrt(jnp.sum(class_f * class_f, axis=1) + epsilon)
    piece = lax.all_gather(shapes, "cls", axis=1, tiled=True)
    term = lax.dot_general(
        piece, classes, (((1,), (1,)), ((), ())), preferred_element_type=jnp.float32
    )
    piece_f = piece.astype(jnp.float32)
    squares = jnp.sum(piece_f * piece_f, axis=1)
    shape_scale = lax.rsqrt(squares + epsilon)
    kernel = jnp.exp(logit_scale * term * shape_scale[:, None] * class_scale[None, :])
    target = counts.astype(jnp.float32)
    row_inv = 1.0 / row_totals(jnp.sum(kernel, axis=1))
    col_scale = jnp.zeros((classes.shape[0],), jnp.float32)
    for step in range(ITERS):
        column_part = jnp.dot(row_inv, kernel, precision=lax.Precision.HIGHEST)
        col_scale = target / lax.psum(column_part, "shape")
        row_inv = 1.0 / row_totals(jnp.dot(kernel, col_scale, precision=lax.Precision.HIGHEST))
    result = row_inv[:, None] * kernel * col_scale[None, :]
    return result.astype(jnp.bfloat16)


def solution(mesh):
    placed = (P("shape", "cls"), P("cls", None), P("cls"))
    return jax.shard_map(
        shards, mesh=mesh, in_specs=placed, out_specs=P("shape", "cls"), check_vma=False
    )
```

profile of v0, /device:TPU:0, one launch (start us, length us, event | category | flops | bytes accessed | tf_op | source)
XLA Modules:
  0.0 246.2 jit_solution(15459654316340277970)
XLA Ops:
  6.5 0.0 all-gather.2.cloned.1.call-start
  6.5 0.7 all-gather.2.cloned.1.call-update
  7.3 7.3 %multiply_reduce_fusion = f32[5120]{0:T(1024)S(1)} fusion(bf16[5120,1280]{1,0:T(8,128)(2,1)} %param.4), kind=kLoop, calls=%fused_computation | loop fusion | flops 19655680 | bytes 13127680 | tf_op jit(solution)/shard_map/reduce_sum | solution.py:17
  14.6 15.2 %all-gather.2.cloned.1.call-done = bf16[512,1280]{0,1:T(8,128)(2,1)} async-done(((bf16[512,320]{0,1:T(8,128)(2,1)}), bf16[512,1280]{0,1:T(8,128)(2,1)}) %all-gather.2.cloned.1.call-update) | async-done | bytes 1310736 | tf_op jit(solution)/shard_map/all_gather | solution.py:18
  29.8 1.7 multiply_reduce_fusion.1
  31.5 16.2 %fusion = (f32[512]{0:T(512)S(1)}, f32[512,5120]{1,0:T(8,128)}) fusion(f32[5120]{0:T(1024)S(1)} %add_rsqrt_fusion, f32[512]{0:T(512)S(1)} %rsqrt_multiply_fusion, bf16[512,1280]{0,1:T(8,128)(2,1)} %all-gather.2.cloned.1.call-done, bf16[5120,1280]{1,0:T(8,128)(2,1)} %param.4), kind=kOutput, calls=%fused_computation.13 | convolution fusion | flops 6718750208 | bytes 24928256 | tf_op jit(solution)/shard_map/dot_general | solution.py:19
  47.7 0.0 copy-start
  47.7 5.9 %psum.49 = f32[512]{0:T(512)S(1)} all-reduce(f32[512]{0:T(512)S(1)} %get-tuple-element.5), channel_id=1, replica_groups=mesh['shape'=8,'cls'=4] {'cls'}, use_global_device_ids=true, to_apply=%region_3.0 | all-reduce | flops 512 | bytes 4096 | tf_op jit(solution)/shard_map/psum | solution.py:12
  53.5 7.6 %fusion.1 = f32[1,5120]{1,0:T(1,128)S(1)} fusion(f32[512,1]{0,1:T(1,128)S(1)} %bitcast.32, f32[512,5120]{1,0:T(8,128)} %get-tuple-element.6), kind=kOutput, calls=%fused_computation.14 | convolution fusion | flops 31457280 | bytes 10508288 | tf_op jit(solution)/shard_map/dot_general | solution.py:30
  61.2 37.2 %psum.50 = f32[5120]{0:T(1024)S(1)} all-reduce(f32[5120]{0:T(1024)S(1)} %bitcast.27), channel_id=1, replica_groups=mesh['shape'=8,'cls'=4] {'shape'}, use_global_device_ids=true, to_apply=%region_4.0 | all-reduce | flops 5120 | bytes 40960 | tf_op jit(solution)/shard_map/psum | solution.py:31
  98.4 0.0 copy-done
  98.4 11.5 %fusion.2 = f32[1,512]{1,0:T(1,128)S(1)} fusion(f32[512,5120]{1,0:T(8,128)} %get-tuple-element.6, f32[5120,1]{0,1:T(1,128)S(1)} %bitcast.30), kind=kOutput, calls=%fused_computation.15 | convolution fusion | flops 31457280 | bytes 10508288 | tf_op jit(solution)/shard_map/dot_general | solution.py:32
  109.9 5.7 %psum.51 = f32[512]{0:T(512)S(1)} all-reduce(f32[512]{0:T(512)S(1)} %bitcast.33), channel_id=1, replica_groups=mesh['shape'=8,'cls'=4] {'cls'}, use_global_device_ids=true, to_apply=%region_5.0 | all-reduce | flops 512 | bytes 4096 | tf_op jit(solution)/shard_map/psum | solution.py:12
  115.6 7.6 %fusion.3 = f32[1,5120]{1,0:T(1,128)S(1)} fusion(f32[512,1]{0,1:T(1,128)S(1)} %bitcast.34, f32[512,5120]{1,0:T(8,128)} %get-tuple-element.6), kind=kOutput, calls=%fused_computation.16 | convolution fusion | flops 31457280 | bytes 10508288 | tf_op jit(solution)/shard_map/dot_general | solution.py:30
  123.2 33.0 %psum.52 = f32[5120]{0:T(1024)S(1)} all-reduce(f32[5120]{0:T(1024)S(1)} %bitcast.28), channel_id=1, replica_groups=mesh['shape'=8,'cls'=4] {'shape'}, use_global_device_ids=true, to_apply=%region_6.0 | all-reduce | flops 5120 | bytes 40960 | tf_op jit(solution)/shard_map/psum | solution.py:31
  156.2 11.5 %fusion.4 = f32[1,512]{1,0:T(1,128)S(1)} fusion(f32[512,5120]{1,0:T(8,128)} %get-tuple-element.6, f32[5120,1]{0,1:T(1,128)S(1)} %bitcast.31), kind=kOutput, calls=%fused_computation.17 | convolution fusion | flops 31457280 | bytes 10508288 | tf_op jit(solution)/shard_map/dot_general | solution.py:32
  167.7 5.9 %psum.53 = f32[512]{0:T(512)S(1)} all-reduce(f32[512]{0:T(512)S(1)} %bitcast.35), channel_id=1, replica_groups=mesh['shape'=8,'cls'=4] {'cls'}, use_global_device_ids=true, to_apply=%region_7.0 | all-reduce | flops 512 | bytes 4096 | tf_op jit(solution)/shard_map/psum | solution.py:12
  173.6 7.6 %fusion.5 = f32[1,5120]{1,0:T(1,128)S(1)} fusion(f32[512,1]{0,1:T(1,128)S(1)} %bitcast.36, f32[512,5120]{1,0:T(8,128)} %get-tuple-element.6), kind=kOutput, calls=%fused_computation.18 | convolution fusion | flops 31457280 | bytes 10508288 | tf_op jit(solution)/shard_map/dot_general | solution.py:30
  181.2 33.0 %psum.54 = f32[5120]{0:T(1024)S(1)} all-reduce(f32[5120]{0:T(1024)S(1)} %bitcast.29), channel_id=1, replica_groups=mesh['shape'=8,'cls'=4] {'shape'}, use_global_device_ids=true, to_apply=%region_8.0 | all-reduce | flops 5120 | bytes 40960 | tf_op jit(solution)/shard_map/psum | solution.py:31
  214.2 11.5 %fusion.6 = f32[1,512]{1,0:T(1,128)S(1)} fusion(f32[512,5120]{1,0:T(8,128)} %get-tuple-element.6, f32[5120,1]{0,1:T(1,128)S(1)} %bitcast.26), kind=kOutput, calls=%fused_computation.19 | convolution fusion | flops 31457280 | bytes 10508288 | tf_op jit(solution)/shard_map/dot_general | solution.py:32
  225.7 5.7 %psum.55 = f32[512]{0:T(512)S(1)} all-reduce(f32[512]{0:T(512)S(1)} %bitcast.37), channel_id=1, replica_groups=mesh['shape'=8,'cls'=4] {'cls'}, use_global_device_ids=true, to_apply=%region_9.0 | all-reduce | flops 512 | bytes 4096 | tf_op jit(solution)/shard_map/psum | solution.py:12
  231.4 8.0 %multiply_convert_fusion = bf16[512,5120]{1,0:T(8,128)(2,1)} fusion(f32[512,5120]{1,0:T(8,128)} %get-tuple-element.6, f32[5120]{0:T(1024)S(1)} %convert_divide_fusion, f32[512]{0:T(512)S(1)} %broadcast_divide_fusion), kind=kLoop, calls=%fused_computation.1 | loop fusion | flops 7864320 | bytes 15751168 | tf_op jit(solution)/shard_map/convert_element_type | solution.py:34
  (9 shorter events, 0.1 us)
Async XLA Ops:
  6.5 23.3 %all-gather.2.cloned.1.call-start = ((), (), s32[]{:S(2)}) async-start(), calls=%async_computation | async-start | bytes 1638400 | tf_op jit(solution)/shard_map/all_gather | solution.py:18
  47.7 50.7 %copy-start = (s32[5120]{0:T(1024)S(1)}, s32[5120]{0:T(1024)}, u32[]{:S(2)}) copy-start(s32[5120]{0:T(1024)} %param.5) | copy-start | bytes 61444
Sparse Core Ops, SparseCore 0:
  8.9 20.8 all-gather.1
where the time goes:
time: 247 us; the launch traced here: 246 us
  blocking collectives  126 us (51%)
  matrix products  73.5 us (30%)
  other arithmetic  17.1 us (7%)
  waiting for transfers between devices  15.9 us (6%)
  between operations  13.4 us (5%)
    psum x3, blocking collectives, shards(): col_scale = target / lax.psum(column_part, 'shape')  103 us
    dot_general x3, matrix products, shards(): jnp.dot(kernel, col_scale, precision=lax.Precision.HIGHEST)  34.4 us
    psum x4, blocking collectives, row_totals(): return lax.psum(partial_value, 'cls')  23 us
    dot_general x3, matrix products, shards(): column_part = jnp.dot(row_inv, kernel, precision=lax.Precision.HIGHEST)  22.9 us
    dot_general x1, matrix products, shards(): lax.dot_general(piece, classes, (((1,), (1,)), ((), ())), preferred_eleme...  16.2 us
    all_gather x1, waiting for transfers between devices, shards(): piece = lax.all_gather(shapes, 'cls', axis=1, tiled=True)  15.2 us
    convert_element_type x1, other arithmetic, shards(): return result.astype(jnp.bfloat16)  8 us
    reduce_sum x1, other arithmetic, shards(): class_scale = lax.rsqrt(jnp.sum(class_f * class_f, axis=1) + epsilon)  7.35 us
  transfers between devices with their start and end apart: 1, of which 1 were waited for; matrix products, arithmetic and copies ran while one was open for 3% of the time, Pallas kernels for 0%

commit v1 on v0

--- a/solution.py
+++ b/solution.py
@@ -15,7 +15,29 @@
 def shards(shapes, classes, counts):
     class_f = classes.astype(jnp.float32)
     class_scale = lax.rsqrt(jnp.sum(class_f * class_f, axis=1) + epsilon)
-    piece = lax.all_gather(shapes, "cls", axis=1, tiled=True)
+    o_now = jax.lax.psum(1, "cls")
+    carry_in, b_now, main = (o_now, jax.lax.axis_index("cls"), shapes.shape[1])
+    val = then = shapes
+    piece = lax.dynamic_update_slice_in_dim(
+        jnp.zeros(
+            tuple((dd * carry_in if dev_i == 1 else dd for dev_i, dd in enumerate(shapes.shape))),
+            shapes.dtype,
+        ),
+        shapes,
+        b_now * main,
+        axis=1,
+    )
+    for i0 in [*range(1, carry_in // 2 + 1)]:
+        val = jax.lax.ppermute(
+            val, "cls", tuple(((dev_i, (dev_i + 1) % carry_in) for dev_i in range(carry_in)))
+        )
+        piece = lax.dynamic_update_slice_in_dim(piece, val, (b_now - i0) % carry_in * main, axis=1)
+        if 2 * i0 < carry_in:
+            h_now = tuple(((dev_i, (dev_i - 1) % carry_in) for dev_i in range(carry_in)))
+            then = jax.lax.ppermute(then, "cls", h_now)
+            piece = lax.dynamic_update_slice_in_dim(
+                piece, then, (b_now + i0) % carry_in * main, axis=1
+            )
     term = lax.dot_general(
         piece, classes, (((1,), (1,)), ((), ())), preferred_element_type=jnp.float32
     )

time: 247 us -> 225 us (0.911)
  between operations: 13.4 us -> 0.13 us
  waiting for transfers between devices: 15.9 us -> 8.25 us
    all_gather x1 -> x0, waiting for transfers between devices: 15.2 us -> none  [shards(): piece = lax.all_gather(shapes, 'cls', axis=1, tiled=True)]
    ppermute x0 -> x3, waiting for transfers between devices: none -> 8.25 us  [the longest x2 8.25 us: shards(): jax.lax.ppermute(val, 'cls', tuple(((dev_i, (dev_i + 1) % carry_in) for d...]
  transfers between devices with their start and end apart: 1 -> 3, of which waited for: 1 -> 2; matrix products, arithmetic and copies ran while one was open for 3% -> 3% of each run, Pallas kernels for 0% -> 0%
where the time goes in v1:
time: 225 us; the launch traced here: 224 us
  blocking collectives  126 us (56%)
  matrix products  71.3 us (32%)
  other arithmetic  15.8 us (7%)
  waiting for transfers between devices  8.25 us (4%)
  starting transfers between devices  2.44 us (1%)
    psum x3, blocking collectives, shards(): col_scale = target / lax.psum(column_part, 'shape')  103 us
    dot_general x3, matrix products, shards(): jnp.dot(kernel, col_scale, precision=lax.Precision.HIGHEST)  34.4 us
    psum x4, blocking collectives, row_totals(): return lax.psum(partial_value, 'cls')  23 us
    dot_general x3, matrix products, shards(): column_part = jnp.dot(row_inv, kernel, precision=lax.Precision.HIGHEST)  22.9 us
    dot_general x1, matrix products, shards(): lax.dot_general(piece, classes, (((1,), (1,)), ((), ())), preferred_eleme...  14 us
    ppermute x2, waiting for transfers between devices, shards(): jax.lax.ppermute(val, 'cls', tuple(((dev_i, (dev_i + 1) % carry_in) for d...  8.25 us
    convert_element_type x1, other arithmetic, shards(): return result.astype(jnp.bfloat16)  8 us
    reduce_sum x1, other arithmetic, shards(): class_scale = lax.rsqrt(jnp.sum(class_f * class_f, axis=1) + epsilon)  7.35 us
  transfers between devices with their start and end apart: 3, of which 2 were waited for; matrix products, arithmetic and copies ran while one was open for 3% of the time, Pallas kernels for 0%

profile of v1, /device:TPU:0, one launch (start us, length us, event | category | flops | bytes accessed | tf_op | source)
XLA Modules:
  0.0 224.4 jit_solution(8693980870699659762)
XLA Ops:
  0.0 2.4 %collective-permute-start.1 = (bf16[512,320]{0,1:T(8,128)(2,1)}, bf16[512,320]{0,1:T(8,128)(2,1)S(1)}, u32[]{:S(2)}, u32[]{:S(2)}) collective-permute-start(bf16[512,320]{0,1:T(8,128)(2,1)} %param.3), channel_id=1, source_target_pairs={{0,3},{1,0},{2,1},{3,2},{4,7},{5,4},{6,5},{7,6},{8,11},{9,8},{10,9... | collective-permute-start | bytes 983048 | tf_op jit(solution)/shard_map/ppermute | solution.py:37
  2.4 0.0 collective-permute-start
  2.4 7.3 %multiply_reduce_fusion = f32[5120]{0:T(1024)S(1)} fusion(bf16[5120,1280]{1,0:T(8,128)(2,1)} %param.4), kind=kLoop, calls=%fused_computation | loop fusion | flops 19655680 | bytes 13127680 | tf_op jit(solution)/shard_map/reduce_sum | solution.py:17
  9.9 2.0 collective-permute-done
  11.8 0.0 collective-permute-start.2
  11.8 0.1 broadcast_in_dim.2
  12.0 0.0 collective-permute-done.1
  12.1 6.3 %collective-permute-done.2 = bf16[512,320]{0,1:T(8,128)(2,1)S(1)} collective-permute-done((bf16[512,320]{0,1:T(8,128)(2,1)S(1)}, bf16[512,320]{0,1:T(8,128)(2,1)S(1)}, u32[]{:S(2)}, u32[]{:S(2)}) %collective-permute-start.2) | collective-permute-done | bytes 327712 | tf_op jit(solution)/shard_map/ppermute | solution.py:31
  18.4 0.3 multiply_reduce_fusion.1
  18.7 14.0 %fusion = (f32[512]{0:T(512)S(1)}, f32[512,5120]{1,0:T(8,128)}) fusion(f32[5120]{0:T(1024)S(1)} %add_rsqrt_fusion, f32[512]{0:T(512)S(1)} %rsqrt_multiply_fusion, bf16[512,1280]{0,1:T(8,128)(2,1)S(1)} %constant_dynamic-update-slice_fusion, bf16[5120,1280]{1,0:T(8,128)(2,1)} %param.4), kind=kOutput, calls=%fused_computation.17 | convolution fusion | flops 6718750208 | bytes 24928256 | tf_op jit(solution)/shard_map/dot_general | solution.py:41
  32.7 5.8 %psum.49 = f32[512]{0:T(512)S(1)} all-reduce(f32[512]{0:T(512)S(1)} %get-tuple-element.5), channel_id=1, replica_groups=mesh['shape'=8,'cls'=4] {'cls'}, use_global_device_ids=true, to_apply=%region_3.4 | all-reduce | flops 512 | bytes 4096 | tf_op jit(solution)/shard_map/psum | solution.py:12
  38.5 7.6 %fusion.1 = f32[1,5120]{1,0:T(1,128)S(1)} fusion(f32[512,1]{0,1:T(1,128)S(1)} %bitcast.32, f32[512,5120]{1,0:T(8,128)} %get-tuple-element.6), kind=kOutput, calls=%fused_computation.18 | convolution fusion | flops 31457280 | bytes 10508288 | tf_op jit(solution)/shard_map/dot_general | solution.py:52
  46.1 37.4 %psum.50 = f32[5120]{0:T(1024)S(1)} all-reduce(f32[5120]{0:T(1024)S(1)} %bitcast.27), channel_id=1, replica_groups=mesh['shape'=8,'cls'=4] {'shape'}, use_global_device_ids=true, to_apply=%region_4.5 | all-reduce | flops 5120 | bytes 40960 | tf_op jit(solution)/shard_map/psum | solution.py:53
  83.5 11.5 %fusion.2 = f32[1,512]{1,0:T(1,128)S(1)} fusion(f32[512,5120]{1,0:T(8,128)} %get-tuple-element.6, f32[5120,1]{0,1:T(1,128)S(1)} %bitcast.30), kind=kOutput, calls=%fused_computation.19 | convolution fusion | flops 31457280 | bytes 10508288 | tf_op jit(solution)/shard_map/dot_general | solution.py:54
  95.0 5.7 %psum.51 = f32[512]{0:T(512)S(1)} all-reduce(f32[512]{0:T(512)S(1)} %bitcast.33), channel_id=1, replica_groups=mesh['shape'=8,'cls'=4] {'cls'}, use_global_device_ids=true, to_apply=%region_5.6 | all-reduce | flops 512 | bytes 4096 | tf_op jit(solution)/shard_map/psum | solution.py:12
  100.6 7.6 %fusion.3 = f32[1,5120]{1,0:T(1,128)S(1)} fusion(f32[512,1]{0,1:T(1,128)S(1)} %bitcast.34, f32[512,5120]{1,0:T(8,128)} %get-tuple-element.6), kind=kOutput, calls=%fused_computation.20 | convolution fusion | flops 31457280 | bytes 10508288 | tf_op jit(solution)/shard_map/dot_general | solution.py:52
  108.3 33.0 %psum.52 = f32[5120]{0:T(1024)S(1)} all-reduce(f32[5120]{0:T(1024)S(1)} %bitcast.28), channel_id=1, replica_groups=mesh['shape'=8,'cls'=4] {'shape'}, use_global_device_ids=true, to_apply=%region_6.7 | all-reduce | flops 5120 | bytes 40960 | tf_op jit(solution)/shard_map/psum | solution.py:53
  141.3 11.5 %fusion.4 = f32[1,512]{1,0:T(1,128)S(1)} fusion(f32[512,5120]{1,0:T(8,128)} %get-tuple-element.6, f32[5120,1]{0,1:T(1,128)S(1)} %bitcast.31), kind=kOutput, calls=%fused_computation.21 | convolution fusion | flops 31457280 | bytes 10508288 | tf_op jit(solution)/shard_map/dot_general | solution.py:54
  152.8 5.9 %psum.53 = f32[512]{0:T(512)S(1)} all-reduce(f32[512]{0:T(512)S(1)} %bitcast.35), channel_id=1, replica_groups=mesh['shape'=8,'cls'=4] {'cls'}, use_global_device_ids=true, to_apply=%region_7.8 | all-reduce | flops 512 | bytes 4096 | tf_op jit(solution)/shard_map/psum | solution.py:12
  158.7 7.6 %fusion.5 = f32[1,5120]{1,0:T(1,128)S(1)} fusion(f32[512,1]{0,1:T(1,128)S(1)} %bitcast.36, f32[512,5120]{1,0:T(8,128)} %get-tuple-element.6), kind=kOutput, calls=%fused_computation.22 | convolution fusion | flops 31457280 | bytes 10508288 | tf_op jit(solution)/shard_map/dot_general | solution.py:52
  166.3 33.0 %psum.54 = f32[5120]{0:T(1024)S(1)} all-reduce(f32[5120]{0:T(1024)S(1)} %bitcast.29), channel_id=1, replica_groups=mesh['shape'=8,'cls'=4] {'shape'}, use_global_device_ids=true, to_apply=%region_8.9 | all-reduce | flops 5120 | bytes 40960 | tf_op jit(solution)/shard_map/psum | solution.py:53
  199.3 11.5 %fusion.6 = f32[1,512]{1,0:T(1,128)S(1)} fusion(f32[512,5120]{1,0:T(8,128)} %get-tuple-element.6, f32[5120,1]{0,1:T(1,128)S(1)} %bitcast.26), kind=kOutput, calls=%fused_computation.23 | convolution fusion | flops 31457280 | bytes 10508288 | tf_op jit(solution)/shard_map/dot_general | solution.py:54
  210.8 5.7 %psum.55 = f32[512]{0:T(512)S(1)} all-reduce(f32[512]{0:T(512)S(1)} %bitcast.37), channel_id=1, replica_groups=mesh['shape'=8,'cls'=4] {'cls'}, use_global_device_ids=true, to_apply=%region_9.10 | all-reduce | flops 512 | bytes 4096 | tf_op jit(solution)/shard_map/psum | solution.py:12
  216.4 8.0 %multiply_convert_fusion = bf16[512,5120]{1,0:T(8,128)(2,1)} fusion(f32[512,5120]{1,0:T(8,128)} %get-tuple-element.6, f32[5120]{0:T(1024)S(1)} %convert_divide_fusion, f32[512]{0:T(512)S(1)} %broadcast_divide_fusion), kind=kLoop, calls=%fused_computation.1 | loop fusion | flops 7864320 | bytes 15751168 | tf_op jit(solution)/shard_map/convert_element_type | solution.py:56
  (17 shorter events, 0.2 us)
Async XLA Ops:
  0.0 11.9 %copy-start = (bf16[512,320]{0,1:T(8,128)(2,1)S(1)}, bf16[512,320]{0,1:T(8,128)(2,1)}, u32[]{:S(2)}) copy-start(bf16[512,320]{0,1:T(8,128)(2,1)} %param.3) | copy-start | bytes 983044
  0.0 12.0 %collective-permute-start.1 = (bf16[512,320]{0,1:T(8,128)(2,1)}, bf16[512,320]{0,1:T(8,128)(2,1)S(1)}, u32[]{:S(2)}, u32[]{:S(2)}) collective-permute-start(bf16[512,320]{0,1:T(8,128)(2,1)} %param.3), channel_id=1, source_target_pairs={{0,3},{1,0},{2,1},{3,2},{4,7},{5,4},{6,5},{7,6},{8,11},{9,8},{10,9... | collective-permute-start | bytes 983048 | tf_op jit(solution)/shard_map/ppermute | solution.py:37
  2.4 9.4 %collective-permute-start = (bf16[512,320]{0,1:T(8,128)(2,1)}, bf16[512,320]{0,1:T(8,128)(2,1)S(1)}, u32[]{:S(2)}, u32[]{:S(2)}) collective-permute-start(bf16[512,320]{0,1:T(8,128)(2,1)} %param.3), channel_id=1, source_target_pairs={{0,1},{1,2},{2,3},{3,0},{4,5},{5,6},{6,7},{7,4},{8,9},{9,10},{10,1... | collective-permute-start | bytes 983048 | tf_op jit(solution)/shard_map/ppermute | solution.py:31
  11.8 6.5 %collective-permute-start.2 = (bf16[512,320]{0,1:T(8,128)(2,1)S(1)}, bf16[512,320]{0,1:T(8,128)(2,1)S(1)}, u32[]{:S(2)}, u32[]{:S(2)}) collective-permute-start(bf16[512,320]{0,1:T(8,128)(2,1)S(1)} %collective-permute-done), channel_id=1, source_target_pairs={{0,1},{1,2},{2,3},{3,0},{4,5},{5,6},{6,7},{7,4},{8,9},{9,10},{10,1... | collective-permute-start | bytes 983048 | tf_op jit(solution)/shard_map/ppermute | solution.py:31
  32.7 50.8 %copy-start.1 = (s32[5120]{0:T(1024)S(1)}, s32[5120]{0:T(1024)}, u32[]{:S(2)}) copy-start(s32[5120]{0:T(1024)} %param.5) | copy-start | bytes 61444
